TPU v7x, 256 devices: a whole 4x4x8 slice. The times are simulated.
256 devices in a mesh: dp: 32 (over y, x, core), expert: 8 (over z).
Axes of the slice: x: 4, y: 4, z: 8, core: 2. Of those that a mesh axis runs over, the one named last changes fastest.
Arguments:
- tokens: bfloat16 [4096, 2048], P('dp'), may hold values from -6 to 6
- route_expert: int32 [4096, 4], P('dp'), may hold values from 0 to 31, all different within a row; in each aligned block of 128 rows (0 to 127, 128 to 255, ...) at most 32 rows name the same one
- route_weight: float32 [4096, 4], P('dp'), may hold values from 0.1 to 1
- gate_weight: bfloat16 [32, 1408, 2048], P('dp', 'expert'), may hold values from -0.125 to 0.125
- up_weight: bfloat16 [32, 1408, 2048], P('dp', 'expert'), may hold values from -0.125 to 0.125
- down_weight: bfloat16 [32, 1408, 2048], P('dp', 'expert'), may hold values from -0.15625 to 0.15625
- gate_scale: float32 [32, 1408], P('dp', 'expert'), may hold values from 0.5 to 2
- up_scale: float32 [32, 1408], P('dp', 'expert'), may hold values from 0.5 to 2
- down_scale: float32 [32, 2048], replicated, may hold values from 0.5 to 2
- cotangent: bfloat16 [4096, 2048], P('dp', 'expert'), may hold values from -6 to 6
Outputs:
- mixed: bfloat16 [4096, 2048], P('dp', 'expert')
- token_grad: bfloat16 [4096, 2048], P('dp', 'expert')
- route_grad: float32 [4096, 4], P('dp')
- gate_grad: float32 [32, 1408, 2048], P('dp', 'expert')
- up_grad: float32 [32, 1408, 2048], P('dp', 'expert')
- down_grad: float32 [32, 1408, 2048], P('dp', 'expert')
Inputs may be any that keep to these rules, and one draw needn't show every extreme that they name: `route_expert`: each row names 4 different experts. Among the 128 rows of one aligned block (the tokens of one index of dp) no expert is named by more than 32 rows, and in some block one expert is named by exactly 32 rows.
All inputs are finite; a program needn't handle non-finite values.
Results may differ from a plain program's by a relative error of at most 0.0058.
Values may be sent and summed in bfloat16 or wider, within the bound.
No kernel may reach another device: no remote copies, remote signals or barrier semaphores. Data moves between devices by JAX's collectives and lax.ppermute only.
A program may use at most 128 MiB of HBM per device.

v0:
```python
import jax
import jax.numpy as jnp
from jax import lax
from jax.sharding import PartitionSpec as P


def local(
    tokens,
    route_expert,
    route_weight,
    gate_weight,
    up_weight,
    down_weight,
    gate_scale,
    up_scale,
    down_scale,
    cotangent,
):
    owners = lax.axis_size("dp")
    tok_rows, width = tokens.shape
    choose = route_expert.shape[1]
    capacity = 2 * tok_rows * choose // owners
    slots = owners * capacity
    assigned = tok_rows * choose
    col_share = width // lax.axis_size("expert")
    col_start = lax.axis_index("expert") * col_share
    flat_expert = route_expert.reshape(-1)
    one_hot = (flat_expert[:, None] == jnp.arange(owners, dtype=jnp.int32)[None, :]).astype(
        jnp.int32
    )
    ranks = jnp.sum((jnp.cumsum(one_hot, axis=0) - 1) * one_hot, axis=1)
    slot_index = flat_expert * capacity + ranks
    slot_token = (
        jnp.zeros((slots,), jnp.int32)
        .at[slot_index]
        .set(jnp.arange(assigned, dtype=jnp.int32) // choose)
    )
    filled = jnp.zeros((slots,), jnp.bool_).at[slot_index].set(True)
    slot_weight = jnp.zeros((slots,), jnp.float32).at[slot_index].set(route_weight.reshape(-1))
    outgoing = jnp.where(
        filled[:, None], jnp.take(tokens, slot_token, axis=0), jnp.zeros((), tokens.dtype)
    )
    arrived = lax.all_to_all(
        outgoing.reshape(owners, capacity, width), "dp", split_axis=0, concat_axis=0, tiled=True
    ).reshape(slots, width)
    gate_local = gate_weight[0]
    up_local = up_weight[0]
    down_local = down_weight[0]
    gate_pre = (
        lax.dot_general(
            arrived, gate_local, (((1,), (1,)), ((), ())), preferred_element_type=jnp.float32
        )
        * gate_scale[0][None, :]
    )
    up_pre = (
        lax.dot_general(
            arrived, up_local, (((1,), (1,)), ((), ())), preferred_element_type=jnp.float32
        )
        * up_scale[0][None, :]
    )
    sigmoid_gate = jax.nn.sigmoid(gate_pre)
    silu_gate = gate_pre * sigmoid_gate
    hidden = (silu_gate * up_pre).astype(jnp.bfloat16)
    summed = lax.psum_scatter(
        lax.dot_general(
            down_local, hidden, (((0,), (1,)), ((), ())), preferred_element_type=jnp.float32
        ),
        "expert",
        scatter_dimension=0,
        tiled=True,
    )
    owner_scale = lax.dynamic_slice(down_scale, (lax.axis_index("dp"), col_start), (1, col_share))[
        0
    ]
    out_cols = (summed * owner_scale[:, None]).astype(jnp.bfloat16)
    returned = lax.all_to_all(
        out_cols.reshape(col_share, owners, capacity), "dp", split_axis=1, concat_axis=1, tiled=True
    ).reshape(col_share, slots)
    picked = (
        jnp.take(returned, slot_index, axis=1)
        .reshape(col_share, tok_rows, choose)
        .astype(jnp.float32)
    )
    mixed = jnp.sum(picked * route_weight[None, :, :], axis=2).T.astype(jnp.bfloat16)
    cot_cols = cotangent.T.astype(jnp.float32)
    route_part = jnp.sum(picked * cot_cols[:, :, None], axis=0)
    route_grad = lax.psum(route_part, "expert")
    slot_scale = jnp.repeat(down_scale, capacity, axis=0)
    full_cot = lax.all_gather(cotangent, "expert", axis=1, tiled=True)
    cot_slots = jnp.take(full_cot, slot_token, axis=0).astype(jnp.float32)
    weighted = (cot_slots * slot_weight[:, None] * slot_scale).astype(jnp.bfloat16)
    out_grad = lax.all_to_all(
        weighted.reshape(owners, capacity, width), "dp", split_axis=0, concat_axis=0, tiled=True
    ).reshape(slots, width)
    hidden_grad = lax.dot_general(
        out_grad, down_local, (((1,), (1,)), ((), ())), preferred_element_type=jnp.float32
    )
    gate_in = (
        hidden_grad
        * up_pre
        * sigmoid_gate
        * (1.0 + gate_pre * (1.0 - sigmoid_gate))
        * gate_scale[0][None, :]
    ).astype(jnp.bfloat16)
    up_in = (hidden_grad * silu_gate * up_scale[0][None, :]).astype(jnp.bfloat16)
    down_grad = lax.dot_general(
        hidden, out_grad, (((0,), (0,)), ((), ())), preferred_element_type=jnp.float32
    )
    gate_grad = lax.dot_general(
        gate_in, arrived, (((0,), (0,)), ((), ())), preferred_element_type=jnp.float32
    )
    up_grad = lax.dot_general(
        up_in, arrived, (((0,), (0,)), ((), ())), preferred_element_type=jnp.float32
    )
    first = lax.dot_general(
        gate_local, gate_in, (((0,), (1,)), ((), ())), preferred_element_type=jnp.float32
    )
    second = lax.dot_general(
        up_local, up_in, (((0,), (1,)), ((), ())), preferred_element_type=jnp.float32
    )
    input_cols = lax.psum_scatter(first + second, "expert", scatter_dimension=0, tiled=True)
    input_home = lax.all_to_all(
        input_cols.reshape(col_share, owners, capacity),
        "dp",
        split_axis=1,
        concat_axis=1,
        tiled=True,
    ).reshape(col_share, slots)
    token_grad = jnp.sum(
        jnp.take(input_home, slot_index, axis=1).reshape(col_share, tok_rows, choose), axis=2
    ).T.astype(jnp.bfloat16)
    return (mixed, token_grad, route_grad, gate_grad[None], up_grad[None], down_grad[None])


def solution(mesh):
    return jax.shard_map(
        local,
        mesh=mesh,
        in_specs=(
            P("dp", None),
            P("dp", None),
            P("dp", None),
            P("dp", "expert", None),
            P("dp", "expert", None),
            P("dp", "expert", None),
            P("dp", "expert"),
            P("dp", "expert"),
            P(),
            P("dp", "expert"),
        ),
        out_specs=(
            P("dp", "expert"),
            P("dp", "expert"),
            P("dp", None),
            P("dp", "expert", None),
            P("dp", "expert", None),
            P("dp", "expert", None),
        ),
        check_vma=False,
    )
```

profile of v0, /device:TPU:2, one launch (start us, length us, event | category | flops | bytes accessed | tf_op | source)
XLA Modules:
  0.0 436.8 jit_solution(8157642740581195982)
XLA Ops:
  10.0 2.4 scatter_custom_fusion.1
  13.3 29.3 %all_gather.3 = bf16[128,2048]{1,0:T(8,128)(2,1)S(1)} all-gather(bf16[128,256]{1,0:T(8,128)(2,1)} %param.21), channel_id=1, replica_groups=mesh['dp'=32,'expert'=8] {'expert'}, dimensions={1}, use_global_device_ids=true | all-gather | bytes 589824 | tf_op jit(solution)/shard_map/all_gather | solution.py:89
  45.1 6.0 %gather_fusion.3 = bf16[1024,2048]{1,0:T(8,128)(2,1)} fusion(bf16[128,2048]{1,0:T(8,128)(2,1)S(1)} %all_gather.3, s32[1024]{0:T(1024)S(1)} %fusion.13), kind=kCustom, calls=%fused_computation.1.clone | custom fusion | bytes 8392704 | tf_op jit(solution)/shard_map/jit(_take)/gather | solution.py:90
  51.2 4.5 %fusion = bf16[1024,2048]{1,0:T(8,128)(2,1)} fusion(bf16[1024,2048]{1,0:T(8,128)(2,1)} %gather_fusion.3, f32[32,2048]{1,0:T(8,128)S(1)} %copy-done.7, f32[1024]{0:T(1024)S(1)} %scatter_custom_fusion.2, pred[1024]{0:T(1024)(128)(4,1)S(1)} %compare_and_fusion.1), kind=kLoop, calls=%fused_computation.8 | loop fusion | flops 10485760 | bytes 8655872 | tf_op jit(solution)/shard_map/convert_element_type | solution.py:91
  55.6 7.8 %all-to-all-start.2 = ((bf16[32,32,2048]{2,1,0:T(8,128)(2,1)}), bf16[32,32,2048]{2,1,0:T(8,128)(2,1)}, u32[]{:S(2)}, u32[]{:S(2)}) async-start(bf16[32,32,2048]{2,1,0:T(8,128)(2,1)} %bitcast.93), calls=%async_computation.3 | async-start | bytes 8388608 | tf_op jit(solution)/shard_map/all_to_all | solution.py:92
  63.4 6.0 %gather_fusion.2 = bf16[1024,2048]{1,0:T(8,128)(2,1)} fusion(bf16[128,2048]{1,0:T(8,128)(2,1)S(1)} %copy-done.1, s32[1024]{0:T(1024)S(1)} %fusion.13), kind=kCustom, calls=%fused_computation.clone | custom fusion | bytes 8392704 | tf_op jit(solution)/shard_map/jit(_take)/gather | solution.py:41
  69.5 2.4 scatter_custom_fusion
  71.9 4.0 select_select_fusion
  75.9 38.9 %all-to-all-done.2 = bf16[32,32,2048]{2,1,0:T(8,128)(2,1)} async-done(((bf16[32,32,2048]{2,1,0:T(8,128)(2,1)}), bf16[32,32,2048]{2,1,0:T(8,128)(2,1)}, u32[]{:S(2)}, u32[]{:S(2)}) %all-to-all-start.2) | async-done | bytes 4194336 | tf_op jit(solution)/shard_map/all_to_all | solution.py:92
  114.9 7.4 %all-to-all-start = ((bf16[32,32,2048]{2,1,0:T(8,128)(2,1)}), bf16[32,32,2048]{2,1,0:T(8,128)(2,1)}, u32[]{:S(2)}, u32[]{:S(2)}) async-start(bf16[32,32,2048]{2,1,0:T(8,128)(2,1)} %bitcast.92), calls=%async_computation | async-start | bytes 8388608 | tf_op jit(solution)/shard_map/all_to_all | solution.py:43
  122.5 4.6 %fusion.1 = f32[1024,176]{0,1:T(8,128)} fusion(bf16[1024,2048]{1,0:T(8,128)(2,1)} %bitcast.18, bf16[1,176,2048]{2,1,0:T(8,128)(2,1)S(1)} %copy-done.5), kind=kOutput, calls=%fused_computation.18 | convolution fusion | flops 738197504 | bytes 5636096 | tf_op jit(solution)/shard_map/dot_general | solution.py:95
  127.1 46.7 %all-to-all-done = bf16[32,32,2048]{2,1,0:T(8,128)(2,1)} async-done(((bf16[32,32,2048]{2,1,0:T(8,128)(2,1)}), bf16[32,32,2048]{2,1,0:T(8,128)(2,1)}, u32[]{:S(2)}, u32[]{:S(2)}) %all-to-all-start) | async-done | bytes 4194336 | tf_op jit(solution)/shard_map/all_to_all | solution.py:43
  173.8 3.8 convolution_multiply_fusion.1
  177.6 4.0 multiply_convert_fusion.3
  182.4 4.5 %convolution_bitcast_fusion = f32[2048,1024]{0,1:T(8,128)} fusion(bf16[1024,176]{0,1:T(8,128)(2,1)S(1)} %get-tuple-element.15, bf16[1,176,2048]{2,1,0:T(8,128)(2,1)S(1)} %copy-done.5), kind=kOutput, calls=%fused_computation.10 | convolution fusion | flops 738197504 | bytes 9469952 | tf_op jit(solution)/shard_map/dot_general | solution.py:65
  188.3 4.5 %add_bitcast_fusion = f32[2048,1024]{0,1:T(8,128)} fusion(f32[1024,2048]{1,0:T(8,128)S(1)} %fusion.6, bf16[1024,176]{0,1:T(8,128)(2,1)S(1)} %get-tuple-element.17, bf16[1,176,2048]{2,1,0:T(8,128)(2,1)S(1)} %copy-done), kind=kOutput, calls=%fused_computation.9 | convolution fusion | flops 740294656 | bytes 17858560 | tf_op jit(solution)/shard_map/dot_general | solution.py:118
  193.0 85.6 %reduce-scatter.3.cloned.1.call-done = f32[256,1024]{0,1:T(8,128)} async-done(((f32[2048,1024]{0,1:T(8,128)}), f32[256,1024]{0,1:T(8,128)}) %reduce-scatter.3.cloned.1.call-update) | async-done | bytes 1048592 | tf_op jit(solution)/shard_map/reduce_scatter | solution.py:64
  280.7 7.4 %all-to-all-start.1 = ((bf16[256,32,32]{0,2,1:T(8,128)(2,1)}), bf16[256,32,32]{0,2,1:T(8,128)(2,1)S(1)}, u32[]{:S(2)}, u32[]{:S(2)}) async-start(bf16[256,32,32]{0,2,1:T(8,128)(2,1)} %bitcast.12), calls=%async_computation.2 | async-start | bytes 1048576 | tf_op jit(solution)/shard_map/all_to_all | solution.py:76
  288.6 86.1 %reduce-scatter.5.cloned.1.call-done = f32[256,1024]{0,1:T(8,128)} async-done(((f32[2048,1024]{0,1:T(8,128)}), f32[256,1024]{0,1:T(8,128)}) %reduce-scatter.5.cloned.1.call-update) | async-done | bytes 1048592 | tf_op jit(solution)/shard_map/reduce_scatter | solution.py:121
  374.7 7.4 %all-to-all-start.3 = ((f32[256,32,32]{0,2,1:T(8,128)}), f32[256,32,32]{0,2,1:T(8,128)S(1)}, u32[]{:S(2)}, u32[]{:S(2)}) async-start(f32[256,32,32]{0,2,1:T(8,128)} %bitcast.97), calls=%async_computation.5 | async-start | bytes 2097152 | tf_op jit(solution)/shard_map/all_to_all | solution.py:122
  382.2 4.3 convolution_bitcast_fusion.1
  386.5 4.3 convolution_bitcast_fusion.3
  390.8 4.2 convolution_bitcast_fusion.2
  397.4 28.7 %psum.7 = f32[128,4]{1,0:T(8,128)S(1)} all-reduce(f32[128,4]{1,0:T(8,128)S(1)} %reduce_sum.48), channel_id=1, replica_groups=mesh['dp'=32,'expert'=8] {'expert'}, use_global_device_ids=true, to_apply=%region_11.13 | all-reduce | flops 512 | bytes 4096 | tf_op jit(solution)/shard_map/psum | solution.py:87
  (67 shorter events, 17.3 us)
Async XLA Ops:
  7.2 170.4 %copy-start = (bf16[1,176,2048]{2,1,0:T(8,128)(2,1)S(1)}, bf16[1,176,2048]{2,1,0:T(8,128)(2,1)}, u32[]{:S(2)}) copy-start(bf16[1,176,2048]{2,1,0:T(8,128)(2,1)} %param.16) | copy-start | bytes 2162692
  45.1 6.0 %copy-start.7 = (f32[32,2048]{1,0:T(8,128)S(1)}, f32[32,2048]{1,0:T(8,128)}, u32[]{:S(2)}) copy-start(f32[32,2048]{1,0:T(8,128)} %param.20) | copy-start | bytes 786436
  55.6 7.8 %copy-start.1 = (bf16[128,2048]{1,0:T(8,128)(2,1)S(1)}, bf16[128,2048]{1,0:T(8,128)(2,1)}, u32[]{:S(2)}) copy-start(bf16[128,2048]{1,0:T(8,128)(2,1)} %param.12) | copy-start | bytes 1572868
  55.6 59.2 %all-to-all-start.2 = ((bf16[32,32,2048]{2,1,0:T(8,128)(2,1)}), bf16[32,32,2048]{2,1,0:T(8,128)(2,1)}, u32[]{:S(2)}, u32[]{:S(2)}) async-start(bf16[32,32,2048]{2,1,0:T(8,128)(2,1)} %bitcast.93), calls=%async_computation.3 | async-start | bytes 8388608 | tf_op jit(solution)/shard_map/all_to_all | solution.py:92
  114.9 7.7 %copy-start.5 = (bf16[1,176,2048]{2,1,0:T(8,128)(2,1)S(1)}, bf16[1,176,2048]{2,1,0:T(8,128)(2,1)}, u32[]{:S(2)}) copy-start(bf16[1,176,2048]{2,1,0:T(8,128)(2,1)} %param.17) | copy-start | bytes 2162692
  114.9 58.9 %all-to-all-start = ((bf16[32,32,2048]{2,1,0:T(8,128)(2,1)}), bf16[32,32,2048]{2,1,0:T(8,128)(2,1)}, u32[]{:S(2)}, u32[]{:S(2)}) async-start(bf16[32,32,2048]{2,1,0:T(8,128)(2,1)} %bitcast.92), calls=%async_computation | async-start | bytes 8388608 | tf_op jit(solution)/shard_map/all_to_all | solution.py:43
  122.3 51.5 %copy-start.6 = (bf16[1,176,2048]{2,1,0:T(8,128)(2,1)S(1)}, bf16[1,176,2048]{2,1,0:T(8,128)(2,1)}, u32[]{:S(2)}) copy-start(bf16[1,176,2048]{2,1,0:T(8,128)(2,1)} %param.15) | copy-start | bytes 2162692
  122.3 51.5 %copy-start.9 = (f32[1,176]{1,0:T(1,128)S(1)}, f32[1,176]{1,0:T(1,128)}, u32[]{:S(2)}) copy-start(f32[1,176]{1,0:T(1,128)} %param.18) | copy-start | bytes 2116
  122.3 156.3 %reduce-scatter.3.cloned.1.call-start = ((), (), s32[]{:S(2)}) async-start(), calls=%async_computation.6 | async-start | bytes 9437184 | tf_op jit(solution)/shard_map/reduce_scatter | solution.py:64
  127.1 50.5 %copy-start.10 = (f32[1,176]{1,0:T(1,128)S(1)}, f32[1,176]{1,0:T(1,128)}, u32[]{:S(2)}) copy-start(f32[1,176]{1,0:T(1,128)} %param.19) | copy-start | bytes 2116
  173.8 3.8 copy-start.11
  181.7 0.7 copy-start.2
  181.7 6.6 %copy-start.3 = (bf16[1024,176]{0,1:T(8,128)(2,1)}, bf16[1024,176]{0,1:T(8,128)(2,1)S(1)}, u32[]{:S(2)}) copy-start(bf16[1024,176]{0,1:T(8,128)(2,1)S(1)} %get-tuple-element.17) | copy-start | bytes 1081348
  186.9 187.8 %reduce-scatter.5.cloned.1.call-start = ((), (), s32[]{:S(2)}) async-start(), calls=%async_computation.7 | async-start | bytes 9437184 | tf_op jit(solution)/shard_map/reduce_scatter | solution.py:121
  192.8 95.5 %copy-start.8 = (bf16[128,256]{1,0:T(8,128)(2,1)S(1)}, bf16[128,256]{1,0:T(8,128)(2,1)}, u32[]{:S(2)}) copy-start(bf16[128,256]{1,0:T(8,128)(2,1)} %param.21) | copy-start | bytes 196612
  280.7 94.0 %all-to-all-start.1 = ((bf16[256,32,32]{0,2,1:T(8,128)(2,1)}), bf16[256,32,32]{0,2,1:T(8,128)(2,1)S(1)}, u32[]{:S(2)}, u32[]{:S(2)}) async-start(bf16[256,32,32]{0,2,1:T(8,128)(2,1)} %bitcast.12), calls=%async_computation.2 | async-start | bytes 1048576 | tf_op jit(solution)/shard_map/all_to_all | solution.py:76
  374.7 52.0 %all-to-all-start.3 = ((f32[256,32,32]{0,2,1:T(8,128)}), f32[256,32,32]{0,2,1:T(8,128)S(1)}, u32[]{:S(2)}, u32[]{:S(2)}) async-start(f32[256,32,32]{0,2,1:T(8,128)} %bitcast.97), calls=%async_computation.5 | async-start | bytes 2097152 | tf_op jit(solution)/shard_map/all_to_all | solution.py:122
  386.5 4.3 copy-start.4
Sparse Core Ops, SparseCore 0:
  187.0 91.5 reduce-scatter.2
  281.1 93.5 reduce-scatter.4
where the time goes:
time: 437 us
  waiting for transfers between devices  257 us (59%)
  blocking collectives  58 us (13%)
  matrix products  35.5 us (8%)
  starting transfers between devices  30.3 us (7%)
  local copies, waits for them, and re-layouts  27.5 us (6%)
  between operations  14.4 us (3%)
  other arithmetic  13.6 us (3%)
    reduce_scatter x1, waiting for transfers between devices, local(): lax.psum_scatter(first + second, 'expert', scatter_dimension=0, tiled=True)  86.1 us
    reduce_scatter x1, waiting for transfers between devices, local(): lax.psum_scatter(lax.dot_general(down_local, hidden, (((0,), (1,)), ((),...  85.6 us
    all_to_all x1, waiting for transfers between devices, local(): lax.all_to_all(outgoing.reshape(owners, capacity, width), 'dp', split_axi...  46.7 us
    all_to_all x1, waiting for transfers between devices, local(): lax.all_to_all(weighted.reshape(owners, capacity, width), 'dp', split_axi...  38.9 us
    all_gather x1, blocking collectives, local(): full_cot = lax.all_gather(cotangent, 'expert', axis=1, tiled=True)  29.3 us
    psum x1, blocking collectives, local(): route_grad = lax.psum(route_part, 'expert')  28.7 us
  transfers between devices with their start and end apart: 6, of which 4 were waited for; matrix products, arithmetic and copies ran while one was open for 9% of the time, Pallas kernels for 0%

commit v1 on v0

--- a/solution.py
+++ b/solution.py
@@ -86,7 +86,12 @@
     route_part = jnp.sum(picked * cot_cols[:, :, None], axis=0)
     route_grad = lax.psum(route_part, "expert")
     slot_scale = jnp.repeat(down_scale, capacity, axis=0)
-    full_cot = lax.all_gather(cotangent, "expert", axis=1, tiled=True)
+    full_cot = jnp.concatenate(
+        jax.lax.all_to_all(
+            jnp.stack([cotangent] * jax.lax.axis_size("expert"), axis=0), "expert", 0, 0
+        ),
+        axis=1,
+    )
     cot_slots = jnp.take(full_cot, slot_token, axis=0).astype(jnp.float32)
     weighted = (cot_slots * slot_weight[:, None] * slot_scale).astype(jnp.bfloat16)
     out_grad = lax.all_to_all(

time: 437 us -> 419 us (0.959)
  blocking collectives: 58 us -> 28.7 us
  starting transfers between devices: 30.3 us -> 38.8 us
    all_gather x1 -> x0, blocking collectives: 29.3 us -> none  [local(): full_cot = lax.all_gather(cotangent, 'expert', axis=1, tiled=True)]
    all_to_all x1, waiting for transfers between devices: 46.7 us -> 38.2 us  [local(): lax.all_to_all(outgoing.reshape(owners, capacity, width), 'dp', split_axi...]
    all_to_all x0 -> x1, starting transfers between devices: none -> 8.47 us  [local(): jax.lax.all_to_all(jnp.stack([cotangent] * jax.lax.axis_size('expert'), a...]
    all_to_all x1, waiting for transfers between devices: 38.9 us -> 46.7 us  [local(): lax.all_to_all(weighted.reshape(owners, capacity, width), 'dp', split_axi...]
  transfers between devices with their start and end apart: 6 -> 7, of which waited for: 4 -> 4; matrix products, arithmetic and copies ran while one was open for 9% -> 14% of each run, Pallas kernels for 0% -> 0%
where the time goes in v1:
time: 419 us
  waiting for transfers between devices  259 us (62%)
  starting transfers between devices  38.8 us (9%)
  matrix products  35.5 us (8%)
  blocking collectives  28.7 us (7%)
  local copies, waits for them, and re-layouts  28.6 us (7%)
  between operations  14.4 us (3%)
  other arithmetic  13.6 us (3%)
    reduce_scatter x1, waiting for transfers between devices, local(): lax.psum_scatter(lax.dot_general(down_local, hidden, (((0,), (1,)), ((),...  88.1 us
    reduce_scatter x1, waiting for transfers between devices, local(): lax.psum_scatter(first + second, 'expert', scatter_dimension=0, tiled=True)  86.2 us
    all_to_all x1, waiting for transfers between devices, local(): lax.all_to_all(weighted.reshape(owners, capacity, width), 'dp', split_axi...  46.7 us
    all_to_all x1, waiting for transfers between devices, local(): lax.all_to_all(outgoing.reshape(owners, capacity, width), 'dp', split_axi...  38.2 us
    psum x1, blocking collectives, local(): route_grad = lax.psum(route_part, 'expert')  28.7 us
    all_to_all x1, starting transfers between devices, local(): jax.lax.all_to_all(jnp.stack([cotangent] * jax.lax.axis_size('expert'), a...  8.47 us
  transfers between devices with their start and end apart: 7, of which 4 were waited for; matrix products, arithmetic and copies ran while one was open for 14% of the time, Pallas kernels for 0%

profile of v1, /device:TPU:2, one launch (start us, length us, event | category | flops | bytes accessed | tf_op | source)
XLA Modules:
  0.0 418.8 jit_solution(3969353077312937151)
XLA Ops:
  9.0 8.5 %all-to-all-start.2 = ((bf16[8,128,256]{2,1,0:T(8,128)(2,1)}), bf16[8,128,256]{2,1,0:T(8,128)(2,1)S(1)}, u32[]{:S(2)}, u32[]{:S(2)}) async-start(bf16[8,128,256]{2,1,0:T(8,128)(2,1)} %stack.2), calls=%async_computation.3 | async-start | bytes 1048576 | tf_op jit(solution)/shard_map/all_to_all | solution.py:90
  20.1 2.4 scatter_custom_fusion.1
  22.6 2.4 scatter_custom_fusion
  25.1 6.0 %gather_fusion.2 = bf16[1024,2048]{1,0:T(8,128)(2,1)} fusion(bf16[128,2048]{1,0:T(8,128)(2,1)S(1)} %copy-done.1, s32[1024]{0:T(1024)S(1)} %fusion.13), kind=kCustom, calls=%fused_computation.clone | custom fusion | bytes 8392704 | tf_op jit(solution)/shard_map/jit(_take)/gather | solution.py:41
  31.1 4.0 select_select_fusion
  35.1 7.8 %all-to-all-start = ((bf16[32,32,2048]{2,1,0:T(8,128)(2,1)}), bf16[32,32,2048]{2,1,0:T(8,128)(2,1)}, u32[]{:S(2)}, u32[]{:S(2)}) async-start(bf16[32,32,2048]{2,1,0:T(8,128)(2,1)} %bitcast.96), calls=%async_computation | async-start | bytes 8388608 | tf_op jit(solution)/shard_map/all_to_all | solution.py:43
  45.7 6.0 %gather_fusion.3 = bf16[1024,2048]{1,0:T(8,128)(2,1)} fusion(bf16[128,2048]{1,0:T(8,128)(2,1)S(1)} %bitcast.94, s32[1024]{0:T(1024)S(1)} %fusion.13), kind=kCustom, calls=%fused_computation.1.clone | custom fusion | bytes 8392704 | tf_op jit(solution)/shard_map/jit(_take)/gather | solution.py:95
  51.7 4.5 %fusion = bf16[1024,2048]{1,0:T(8,128)(2,1)} fusion(bf16[1024,2048]{1,0:T(8,128)(2,1)} %gather_fusion.3, f32[32,2048]{1,0:T(8,128)S(1)} %copy-done.7, f32[1024]{0:T(1024)S(1)} %scatter_custom_fusion.2, pred[1024]{0:T(1024)(128)(4,1)S(1)} %compare_and_fusion.1), kind=kLoop, calls=%fused_computation.8 | loop fusion | flops 10485760 | bytes 8655872 | tf_op jit(solution)/shard_map/convert_element_type | solution.py:96
  56.2 38.2 %all-to-all-done = bf16[32,32,2048]{2,1,0:T(8,128)(2,1)} async-done(((bf16[32,32,2048]{2,1,0:T(8,128)(2,1)}), bf16[32,32,2048]{2,1,0:T(8,128)(2,1)}, u32[]{:S(2)}, u32[]{:S(2)}) %all-to-all-start) | async-done | bytes 4194336 | tf_op jit(solution)/shard_map/all_to_all | solution.py:43
  94.4 7.4 %all-to-all-start.3 = ((bf16[32,32,2048]{2,1,0:T(8,128)(2,1)}), bf16[32,32,2048]{2,1,0:T(8,128)(2,1)}, u32[]{:S(2)}, u32[]{:S(2)}) async-start(bf16[32,32,2048]{2,1,0:T(8,128)(2,1)} %bitcast.97), calls=%async_computation.4 | async-start | bytes 8388608 | tf_op jit(solution)/shard_map/all_to_all | solution.py:97
  102.1 4.6 %convolution_multiply_fusion.1 = f32[1024,176]{0,1:T(8,128)} fusion(bf16[1024,2048]{1,0:T(8,128)(2,1)} %bitcast.4, bf16[1,176,2048]{2,1,0:T(8,128)(2,1)S(1)} %copy-done.6, f32[176]{0:T(256)S(1)} %bitcast.111), kind=kOutput, calls=%fused_computation.16 | convolution fusion | flops 738377728 | bytes 5636800 | tf_op jit(solution)/shard_map/dot_general | solution.py:50
  106.6 46.7 %all-to-all-done.3 = bf16[32,32,2048]{2,1,0:T(8,128)(2,1)} async-done(((bf16[32,32,2048]{2,1,0:T(8,128)(2,1)}), bf16[32,32,2048]{2,1,0:T(8,128)(2,1)}, u32[]{:S(2)}, u32[]{:S(2)}) %all-to-all-start.3) | async-done | bytes 4194336 | tf_op jit(solution)/shard_map/all_to_all | solution.py:97
  153.3 3.8 fusion.1
  157.1 4.0 multiply_convert_fusion.3
  161.9 4.5 %convolution_bitcast_fusion = f32[2048,1024]{0,1:T(8,128)} fusion(bf16[1024,176]{0,1:T(8,128)(2,1)S(1)} %get-tuple-element.21, bf16[1,176,2048]{2,1,0:T(8,128)(2,1)S(1)} %copy-done.5), kind=kOutput, calls=%fused_computation.10 | convolution fusion | flops 738197504 | bytes 9469952 | tf_op jit(solution)/shard_map/dot_general | solution.py:65
  167.8 4.5 %add_bitcast_fusion = f32[2048,1024]{0,1:T(8,128)} fusion(f32[1024,2048]{1,0:T(8,128)S(1)} %fusion.6, bf16[1024,176]{0,1:T(8,128)(2,1)S(1)} %get-tuple-element.23, bf16[1,176,2048]{2,1,0:T(8,128)(2,1)S(1)} %copy-done), kind=kOutput, calls=%fused_computation.9 | convolution fusion | flops 740294656 | bytes 17858560 | tf_op jit(solution)/shard_map/dot_general | solution.py:123
  172.5 88.1 %reduce-scatter.3.cloned.1.call-done = f32[256,1024]{0,1:T(8,128)} async-done(((f32[2048,1024]{0,1:T(8,128)}), f32[256,1024]{0,1:T(8,128)}) %reduce-scatter.3.cloned.1.call-update) | async-done | bytes 1048592 | tf_op jit(solution)/shard_map/reduce_scatter | solution.py:64
  262.7 7.4 %all-to-all-start.1 = ((bf16[256,32,32]{0,2,1:T(8,128)(2,1)}), bf16[256,32,32]{0,2,1:T(8,128)(2,1)S(1)}, u32[]{:S(2)}, u32[]{:S(2)}) async-start(bf16[256,32,32]{0,2,1:T(8,128)(2,1)} %bitcast.12), calls=%async_computation.2 | async-start | bytes 1048576 | tf_op jit(solution)/shard_map/all_to_all | solution.py:76
  270.6 86.2 %reduce-scatter.5.cloned.1.call-done = f32[256,1024]{0,1:T(8,128)} async-done(((f32[2048,1024]{0,1:T(8,128)}), f32[256,1024]{0,1:T(8,128)}) %reduce-scatter.5.cloned.1.call-update) | async-done | bytes 1048592 | tf_op jit(solution)/shard_map/reduce_scatter | solution.py:126
  356.8 7.4 %all-to-all-start.4 = ((f32[256,32,32]{0,2,1:T(8,128)}), f32[256,32,32]{0,2,1:T(8,128)S(1)}, u32[]{:S(2)}, u32[]{:S(2)}) async-start(f32[256,32,32]{0,2,1:T(8,128)} %bitcast.102), calls=%async_computation.6 | async-start | bytes 2097152 | tf_op jit(solution)/shard_map/all_to_all | solution.py:127
  364.2 4.3 %convolution_bitcast_fusion.1 = f32[1,176,2048]{2,1,0:T(8,128)} fusion(bf16[1024,176]{0,1:T(8,128)(2,1)} %copy-done.2, bf16[1024,2048]{1,0:T(8,128)(2,1)} %bitcast.19), kind=kOutput, calls=%fused_computation.12 | convolution fusion | flops 738197504 | bytes 5996544 | tf_op jit(solution)/shard_map/dot_general | solution.py:111
  368.5 4.3 %convolution_bitcast_fusion.3 = f32[1,176,2048]{2,1,0:T(8,128)} fusion(bf16[1024,176]{0,1:T(8,128)(2,1)S(1)} %get-tuple-element.22, bf16[1024,2048]{1,0:T(8,128)(2,1)} %bitcast.4), kind=kOutput, calls=%fused_computation.14 | convolution fusion | flops 738197504 | bytes 5996544 | tf_op jit(solution)/shard_map/dot_general | solution.py:114
  372.8 4.2 %convolution_bitcast_fusion.2 = f32[1,176,2048]{2,1,0:T(8,128)} fusion(bf16[1024,176]{0,1:T(8,128)(2,1)S(1)} %copy-done.4, bf16[1024,2048]{1,0:T(8,128)(2,1)} %bitcast.4), kind=kOutput, calls=%fused_computation.13 | convolution fusion | flops 738197504 | bytes 5996544 | tf_op jit(solution)/shard_map/dot_general | solution.py:117
  379.4 28.7 %psum.7 = f32[128,4]{1,0:T(8,128)S(1)} all-reduce(f32[128,4]{1,0:T(8,128)S(1)} %reduce_sum.48), channel_id=1, replica_groups=mesh['dp'=32,'expert'=8] {'expert'}, use_global_device_ids=true, to_apply=%region_11.13 | all-reduce | flops 512 | bytes 4096 | tf_op jit(solution)/shard_map/psum | solution.py:87
  (72 shorter events, 18.4 us)
Async XLA Ops:
  7.2 150.0 %copy-start = (bf16[1,176,2048]{2,1,0:T(8,128)(2,1)S(1)}, bf16[1,176,2048]{2,1,0:T(8,128)(2,1)}, u32[]{:S(2)}) copy-start(bf16[1,176,2048]{2,1,0:T(8,128)(2,1)} %param.16) | copy-start | bytes 2162692
  7.2 17.9 %copy-start.1 = (bf16[128,2048]{1,0:T(8,128)(2,1)S(1)}, bf16[128,2048]{1,0:T(8,128)(2,1)}, u32[]{:S(2)}) copy-start(bf16[128,2048]{1,0:T(8,128)(2,1)} %param.12) | copy-start | bytes 1572868
  9.0 26.2 %all-to-all-start.2 = ((bf16[8,128,256]{2,1,0:T(8,128)(2,1)}), bf16[8,128,256]{2,1,0:T(8,128)(2,1)S(1)}, u32[]{:S(2)}, u32[]{:S(2)}) async-start(bf16[8,128,256]{2,1,0:T(8,128)(2,1)} %stack.2), calls=%async_computation.3 | async-start | bytes 1048576 | tf_op jit(solution)/shard_map/all_to_all | solution.py:90
  35.1 7.8 %copy-start.9 = (f32[128,4]{0,1:T(4,128)S(1)}, f32[128,4]{0,1:T(4,128)}, u32[]{:S(2)}) copy-start(f32[128,4]{0,1:T(4,128)} %param.14) | copy-start | bytes 6148
  35.1 59.2 %all-to-all-start = ((bf16[32,32,2048]{2,1,0:T(8,128)(2,1)}), bf16[32,32,2048]{2,1,0:T(8,128)(2,1)}, u32[]{:S(2)}, u32[]{:S(2)}) async-start(bf16[32,32,2048]{2,1,0:T(8,128)(2,1)} %bitcast.96), calls=%async_computation | async-start | bytes 8388608 | tf_op jit(solution)/shard_map/all_to_all | solution.py:43
  45.7 6.0 %copy-start.7 = (f32[32,2048]{1,0:T(8,128)S(1)}, f32[32,2048]{1,0:T(8,128)}, u32[]{:S(2)}) copy-start(f32[32,2048]{1,0:T(8,128)} %param.20) | copy-start | bytes 786436
  94.4 7.7 %copy-start.6 = (bf16[1,176,2048]{2,1,0:T(8,128)(2,1)S(1)}, bf16[1,176,2048]{2,1,0:T(8,128)(2,1)}, u32[]{:S(2)}) copy-start(bf16[1,176,2048]{2,1,0:T(8,128)(2,1)} %param.15) | copy-start | bytes 2162692
  94.4 7.7 %copy-start.10 = (f32[1,176]{1,0:T(1,128)S(1)}, f32[1,176]{1,0:T(1,128)}, u32[]{:S(2)}) copy-start(f32[1,176]{1,0:T(1,128)} %param.18) | copy-start | bytes 2116
  94.4 58.9 %all-to-all-start.3 = ((bf16[32,32,2048]{2,1,0:T(8,128)(2,1)}), bf16[32,32,2048]{2,1,0:T(8,128)(2,1)}, u32[]{:S(2)}, u32[]{:S(2)}) async-start(bf16[32,32,2048]{2,1,0:T(8,128)(2,1)} %bitcast.97), calls=%async_computation.4 | async-start | bytes 8388608 | tf_op jit(solution)/shard_map/all_to_all | solution.py:97
  101.8 51.5 %copy-start.5 = (bf16[1,176,2048]{2,1,0:T(8,128)(2,1)S(1)}, bf16[1,176,2048]{2,1,0:T(8,128)(2,1)}, u32[]{:S(2)}) copy-start(bf16[1,176,2048]{2,1,0:T(8,128)(2,1)} %param.17) | copy-start | bytes 2162692
  101.8 158.8 %reduce-scatter.3.cloned.1.call-start = ((), (), s32[]{:S(2)}) async-start(), calls=%async_computation.7 | async-start | bytes 9437184 | tf_op jit(solution)/shard_map/reduce_scatter | solution.py:64
  106.6 50.5 %copy-start.11 = (f32[1,176]{1,0:T(1,128)S(1)}, f32[1,176]{1,0:T(1,128)}, u32[]{:S(2)}) copy-start(f32[1,176]{1,0:T(1,128)} %param.19) | copy-start | bytes 2116
  153.3 3.8 copy-start.12
  161.2 0.7 copy-start.2
  161.2 6.6 %copy-start.3 = (bf16[1024,176]{0,1:T(8,128)(2,1)}, bf16[1024,176]{0,1:T(8,128)(2,1)S(1)}, u32[]{:S(2)}) copy-start(bf16[1024,176]{0,1:T(8,128)(2,1)S(1)} %get-tuple-element.23) | copy-start | bytes 1081348
  166.4 190.3 %reduce-scatter.5.cloned.1.call-start = ((), (), s32[]{:S(2)}) async-start(), calls=%async_computation.8 | async-start | bytes 9437184 | tf_op jit(solution)/shard_map/reduce_scatter | solution.py:126
  172.3 98.0 %copy-start.8 = (bf16[128,256]{1,0:T(8,128)(2,1)S(1)}, bf16[128,256]{1,0:T(8,128)(2,1)}, u32[]{:S(2)}) copy-start(bf16[128,256]{1,0:T(8,128)(2,1)} %param.21) | copy-start | bytes 196612
  262.7 94.1 %all-to-all-start.1 = ((bf16[256,32,32]{0,2,1:T(8,128)(2,1)}), bf16[256,32,32]{0,2,1:T(8,128)(2,1)S(1)}, u32[]{:S(2)}, u32[]{:S(2)}) async-start(bf16[256,32,32]{0,2,1:T(8,128)(2,1)} %bitcast.12), calls=%async_computation.2 | async-start | bytes 1048576 | tf_op jit(solution)/shard_map/all_to_all | solution.py:76
  356.8 52.0 %all-to-all-start.4 = ((f32[256,32,32]{0,2,1:T(8,128)}), f32[256,32,32]{0,2,1:T(8,128)S(1)}, u32[]{:S(2)}, u32[]{:S(2)}) async-start(f32[256,32,32]{0,2,1:T(8,128)} %bitcast.102), calls=%async_computation.6 | async-start | bytes 2097152 | tf_op jit(solution)/shard_map/all_to_all | solution.py:127
  368.5 4.3 %copy-start.4 = (bf16[1024,176]{0,1:T(8,128)(2,1)S(1)}, bf16[1024,176]{0,1:T(8,128)(2,1)}, u32[]{:S(2)}) copy-start(bf16[1024,176]{0,1:T(8,128)(2,1)} %copy-done.3) | copy-start | bytes 1081348
Sparse Core Ops, SparseCore 0:
  166.6 93.9 reduce-scatter.2
  263.1 93.5 reduce-scatter.4
